TPU v7x, 32 devices: a whole 2x2x4 slice. The times are simulated.
32 devices in a mesh: seq: 2 (over core), narrow: 4 (over y, x), wide: 4 (over z).
Axes of the slice: x: 2, y: 2, z: 4, core: 2. Of those that a mesh axis runs over, the one named last changes fastest.
Arguments:
- tokens: bfloat16 [8192, 2048], P('seq', 'narrow'), may hold values from -6 to 6
- attn_gain: float32 [2048], P('narrow'), may hold values from 0.5 to 1.5
- w_query: bfloat16 [2048, 2048], P('narrow', 'wide'), may hold values from -0.125 to 0.125
- w_key: bfloat16 [2048, 512], P('narrow', 'wide'), may hold values from -0.125 to 0.125
- w_value: bfloat16 [2048, 512], P('narrow', 'wide'), may hold values from -0.125 to 0.125
- w_out: bfloat16 [2048, 2048], P('wide', 'narrow'), may hold values from -2 to 2
- ffn_gain: float32 [2048], P('narrow'), may hold values from 0.5 to 1.5
- w_gate: bfloat16 [2048, 8192], P('narrow', 'wide'), may hold values from -0.125 to 0.125
- w_up: bfloat16 [2048, 8192], P('narrow', 'wide'), may hold values from -0.125 to 0.125
- w_down: bfloat16 [8192, 2048], P('wide', 'narrow'), may hold values from -0.0625 to 0.0625
- segment_ids: int32 [8192], replicated, may hold values from 0 to 2, as said below
- token_mask: int32 [8192], replicated, may hold values from 0 to 1, as said below
- out_grad: bfloat16 [8192, 2048], P('seq', 'narrow'), may hold values from -6 to 6
Outputs:
- result: bfloat16 [8192, 2048], P('seq', 'narrow')
- input_grad: float32 [8192, 2048], P('seq', 'narrow')
- grad_attn_gain: float32 [2048], P('narrow')
- grad_w_query: float32 [2048, 2048], P('narrow', 'wide')
- grad_w_key: float32 [2048, 512], P('narrow', 'wide')
- grad_w_value: float32 [2048, 512], P('narrow', 'wide')
- grad_w_out: float32 [2048, 2048], P('wide', 'narrow')
- grad_ffn_gain: float32 [2048], P('narrow')
- grad_w_gate: float32 [2048, 8192], P('narrow', 'wide')
- grad_w_up: float32 [2048, 8192], P('narrow', 'wide')
- grad_w_down: float32 [8192, 2048], P('wide', 'narrow')
Inputs may be any that keep to these rules, and one draw needn't show every extreme that they name: `segment_ids`: the pack holds three sequences in order, ids 0, 1, 2, never falling: the first and the last hold 2 to 256 positions each, the middle one all the rest. `token_mask`: padding is the last positions of each sequence: 1 to 255 of the middle one; of the first and the last, one or more and fewer than the sequence's length; the first position of each sequence is a real token.
All inputs are finite; a program needn't handle non-finite values.
Results may differ from a plain program's by a relative error of at most 0.018.
Values may be sent and summed in bfloat16 or wider, within the bound.
A program may use at most 384 MiB of HBM per device.

v0:
```python
import jax
import jax.numpy as jnp
from jax import lax
from jax.sharding import PartitionSpec as P

D = 2048
HD = 64
EPS = 1e-05
THETA = 500000.0
NEG = -1e30


def positions(segment_ids):
    token_index = jnp.arange(segment_ids.shape[0], dtype=jnp.int32)
    seg_first = jnp.concatenate([jnp.ones((1,), dtype=bool), segment_ids[1:] != segment_ids[:-1]])
    seg_start = lax.cummax(jnp.where(seg_first, token_index, jnp.zeros_like(token_index)), axis=0)
    return token_index - seg_start


def rotation(token_pos):
    half_dim = HD // 2
    frequency = THETA ** (-2.0 * jnp.arange(half_dim, dtype=jnp.float32) / HD)
    angles = token_pos.astype(jnp.float32)[:, None] * frequency[None, :]
    cosine_table = jnp.concatenate([jnp.cos(angles), jnp.cos(angles)], axis=1)
    sine_table = jnp.concatenate([jnp.sin(angles), jnp.sin(angles)], axis=1)
    return (cosine_table, sine_table)


def rotate(vectors, cosine_table, sine_table, turn_sign):
    half_dim = HD // 2
    turned = jnp.concatenate([-vectors[..., half_dim:], vectors[..., :half_dim]], axis=-1)
    return vectors * cosine_table[:, None, :] + turn_sign * turned * sine_table[:, None, :]


def narrow_total(values):
    return lax.psum(values, "narrow")


def wide_total(values):
    return lax.psum(values, "wide")


def gather_rows(values):
    return lax.all_gather(values, "narrow", axis=0, tiled=True)


def rms_norm(values):
    squares = narrow_total(jnp.sum(values * values, axis=1))
    row_scale = lax.rsqrt(squares / D + EPS)
    return (values * row_scale[:, None], row_scale)


def norm_back(grad_h, normed, row_scale, gain_vec):
    grad_normed = grad_h * gain_vec[None, :]
    inner_sum = narrow_total(jnp.sum(grad_normed * normed, axis=1))
    grad_input = row_scale[:, None] * (grad_normed - normed * (inner_sum / D)[:, None])
    return (grad_input, jnp.sum(grad_h * normed, axis=0))


def sum_rows(left_side, weight, product_kind):

    def term_rows():
        if product_kind == "flip":
            return lax.dot_general(
                left_side, weight, (((1,), (1,)), ((), ())), preferred_element_type=jnp.float32
            )
        return jnp.dot(left_side, weight, preferred_element_type=jnp.float32)

    return lax.psum_scatter(term_rows(), "narrow", scatter_dimension=0, tiled=True)


def back_rows(grad_rows, weight, inputs):
    shard_piece = lax.all_gather(grad_rows, "narrow", axis=0, tiled=True)
    product = lax.dot_general(
        shard_piece, weight, (((1,), (1,)), ((), ())), preferred_element_type=jnp.float32
    )
    weight_grad = lax.dot_general(
        inputs, shard_piece, (((0,), (0,)), ((), ())), preferred_element_type=jnp.float32
    )
    return (product, weight_grad)


def body(
    tokens,
    attn_gain,
    w_query,
    w_key,
    w_value,
    w_out,
    ffn_gain,
    w_gate,
    w_up,
    w_down,
    segment_ids,
    token_mask,
    out_grad,
):
    narrow_count = lax.axis_size("narrow")
    tok_count = tokens.shape[0]
    quarter = tok_count // narrow_count
    total_tokens = segment_ids.shape[0]
    seq_index = lax.axis_index("seq")
    narrow_index = lax.axis_index("narrow")
    q_width = w_query.shape[1]
    kv_width = w_key.shape[1]
    q_heads = q_width // HD
    kv_heads = kv_width // HD
    group_size = q_heads // kv_heads
    ff_width = w_gate.shape[1]
    score_scale = HD ** (-0.5)
    cosine_all, sine_all = rotation(positions(segment_ids))
    own_first = seq_index * tok_count + narrow_index * quarter
    own_index = own_first + jnp.arange(quarter, dtype=jnp.int32)
    cosine_table = lax.dynamic_slice_in_dim(cosine_all, own_first, quarter, 0)
    sine_table = lax.dynamic_slice_in_dim(sine_all, own_first, quarter, 0)
    own_segment = lax.dynamic_slice_in_dim(segment_ids, own_first, quarter, 0)
    key_index = jnp.arange(total_tokens, dtype=jnp.int32)
    allowed = (
        (own_segment[:, None] == segment_ids[None, :])
        & (key_index[None, :] <= own_index[:, None])
        & (token_mask[None, :] == 1)
    )
    row_valid = lax.dynamic_slice_in_dim(token_mask, seq_index * tok_count, tok_count, 0)
    grad_low = jnp.where(row_valid[:, None] == 1, out_grad, jnp.zeros_like(out_grad))
    grad_float = grad_low.astype(jnp.float32)
    x_float = tokens.astype(jnp.float32)
    normed_one, scale_one = rms_norm(x_float)
    h_one = (normed_one * attn_gain[None, :]).astype(jnp.bfloat16)
    w_qkv = jnp.concatenate([w_query, w_key, w_value], axis=1)
    qkv_lin = sum_rows(h_one, w_qkv, "plain")
    query_rot = rotate(
        qkv_lin[:, :q_width].reshape(quarter, q_heads, HD), cosine_table, sine_table, 1.0
    ).astype(jnp.bfloat16)
    key_rot = rotate(
        qkv_lin[:, q_width : q_width + kv_width].reshape(quarter, kv_heads, HD),
        cosine_table,
        sine_table,
        1.0,
    ).astype(jnp.bfloat16)
    value_low = qkv_lin[:, q_width + kv_width :].astype(jnp.bfloat16)
    kv_local = jnp.concatenate([key_rot.reshape(quarter, kv_width), value_low], axis=1)
    kv_all = lax.all_gather(kv_local, ("seq", "narrow"), axis=0, tiled=True)
    keys_all = kv_all[:, :kv_width].reshape(total_tokens, kv_heads, HD)
    values_all = kv_all[:, kv_width:].reshape(total_tokens, kv_heads, HD)
    query_heads = jnp.transpose(query_rot, (1, 0, 2))
    head_ids = jnp.arange(q_heads, dtype=jnp.int32)

    def head_scores(query_one, head_id):
        kv_id = head_id // group_size
        key_one = lax.dynamic_index_in_dim(keys_all, kv_id, 1, keepdims=False)
        value_one = lax.dynamic_index_in_dim(values_all, kv_id, 1, keepdims=False)
        scores = (
            lax.dot_general(
                query_one, key_one, (((1,), (1,)), ((), ())), preferred_element_type=jnp.float32
            )
            * score_scale
        )
        return (jnp.where(allowed, scores, NEG), key_one, value_one)

    def head_forward(packed):
        query_one, head_id = packed
        scores, key_one, value_one = head_scores(query_one, head_id)
        row_top = jnp.max(scores, axis=1, keepdims=True)
        log_total = row_top + jnp.log(jnp.sum(jnp.exp(scores - row_top), axis=1, keepdims=True))
        prob_low = jnp.exp(scores - log_total).astype(jnp.bfloat16)
        return (jnp.dot(prob_low, value_one, preferred_element_type=jnp.float32), log_total[:, 0])

    head_out, log_totals = lax.map(head_forward, (query_heads, head_ids))
    attn_heads = jnp.transpose(head_out, (1, 0, 2)).reshape(quarter, q_width).astype(jnp.bfloat16)
    attn_all = gather_rows(attn_heads)
    middle = x_float + wide_total(jnp.dot(attn_all, w_out, preferred_element_type=jnp.float32))
    normed_two, scale_two = rms_norm(middle)
    h_two = (normed_two * ffn_gain[None, :]).astype(jnp.bfloat16)
    w_gate_up = jnp.concatenate([w_gate, w_up], axis=1)
    gate_up = sum_rows(h_two, w_gate_up, "plain")
    gate_lin = gate_up[:, :ff_width]
    up_lin = gate_up[:, ff_width:]
    gate_sig = jax.nn.sigmoid(gate_lin)
    act_low = (gate_lin * gate_sig * up_lin).astype(jnp.bfloat16)
    act_all = gather_rows(act_low)
    down_sum = wide_total(jnp.dot(act_all, w_down, preferred_element_type=jnp.float32))
    result = (middle + down_sum).astype(jnp.bfloat16)
    grad_w_down = lax.dot_general(
        act_all, grad_low, (((0,), (0,)), ((), ())), preferred_element_type=jnp.float32
    )
    act_grad = sum_rows(grad_low, w_down, "flip")
    gate_grad = act_grad * up_lin * gate_sig * (1.0 + gate_lin * (1.0 - gate_sig))
    up_grad = act_grad * gate_lin * gate_sig
    gate_up_grad = jnp.concatenate([gate_grad, up_grad], axis=1).astype(jnp.bfloat16)
    middle_part, grad_gate_up = back_rows(gate_up_grad, w_gate_up, h_two)
    middle_norm_grad, grad_ffn_gain = norm_back(
        wide_total(middle_part), normed_two, scale_two, ffn_gain
    )
    middle_grad = grad_float + middle_norm_grad
    attn_grad_low = middle_grad.astype(jnp.bfloat16)
    grad_w_out = lax.dot_general(
        attn_all, attn_grad_low, (((0,), (0,)), ((), ())), preferred_element_type=jnp.float32
    )
    heads_grad = sum_rows(attn_grad_low, w_out, "flip").astype(jnp.bfloat16)
    heads_grad_split = jnp.transpose(heads_grad.reshape(quarter, q_heads, HD), (1, 0, 2))

    def head_backward(packed):
        query_one, grad_one, log_total, head_id = packed
        scores, key_one, value_one = head_scores(query_one, head_id)
        attn_prob = jnp.exp(scores - log_total[:, None])
        prob_low = attn_prob.astype(jnp.bfloat16)
        prob_grad = lax.dot_general(
            grad_one, value_one, (((1,), (1,)), ((), ())), preferred_element_type=jnp.float32
        )
        inner_sum = jnp.sum(attn_prob * prob_grad, axis=1, keepdims=True)
        score_grad = (attn_prob * (prob_grad - inner_sum)).astype(jnp.bfloat16)
        query_grad = jnp.dot(score_grad, key_one, preferred_element_type=jnp.float32) * score_scale
        key_grad = (
            lax.dot_general(
                score_grad, query_one, (((0,), (0,)), ((), ())), preferred_element_type=jnp.float32
            )
            * score_scale
        )
        value_grad = lax.dot_general(
            prob_low, grad_one, (((0,), (0,)), ((), ())), preferred_element_type=jnp.float32
        )
        return (query_grad, key_grad, value_grad)

    query_grads, key_grads, value_grads = lax.map(
        head_backward, (query_heads, heads_grad_split, log_totals, head_ids)
    )
    key_sum = jnp.sum(key_grads.reshape(kv_heads, group_size, total_tokens, HD), axis=1)
    value_sum = jnp.sum(value_grads.reshape(kv_heads, group_size, total_tokens, HD), axis=1)
    kv_grad_all = jnp.concatenate(
        [
            jnp.transpose(key_sum, (1, 0, 2)).reshape(total_tokens, kv_width),
            jnp.transpose(value_sum, (1, 0, 2)).reshape(total_tokens, kv_width),
        ],
        axis=1,
    )
    kv_grad = lax.psum_scatter(
        kv_grad_all.astype(jnp.bfloat16), ("seq", "narrow"), scatter_dimension=0, tiled=True
    ).astype(jnp.float32)
    query_back = rotate(
        jnp.transpose(query_grads, (1, 0, 2)), cosine_table, sine_table, -1.0
    ).reshape(quarter, q_width)
    key_back = rotate(
        kv_grad[:, :kv_width].reshape(quarter, kv_heads, HD), cosine_table, sine_table, -1.0
    ).reshape(quarter, kv_width)
    qkv_grad = jnp.concatenate([query_back, key_back, kv_grad[:, kv_width:]], axis=1).astype(
        jnp.bfloat16
    )
    first_part, grad_qkv = back_rows(qkv_grad, w_qkv, h_one)
    input_part, grad_attn_gain = norm_back(wide_total(first_part), normed_one, scale_one, attn_gain)
    input_grad = middle_grad + input_part
    summed = (
        lax.psum(grad_attn_gain.astype(jnp.bfloat16), "seq").astype(jnp.float32),
        lax.psum(grad_qkv.astype(jnp.bfloat16), "seq").astype(jnp.float32),
        lax.psum(grad_w_out.astype(jnp.bfloat16), "seq").astype(jnp.float32),
        lax.psum(grad_ffn_gain.astype(jnp.bfloat16), "seq").astype(jnp.float32),
        lax.psum(grad_gate_up.astype(jnp.bfloat16), "seq").astype(jnp.float32),
        lax.psum(grad_w_down.astype(jnp.bfloat16), "seq").astype(jnp.float32),
    )
    qkv_total = summed[1]
    gate_up_total = summed[4]
    return (
        result,
        input_grad,
        summed[0],
        qkv_total[:, :q_width],
        qkv_total[:, q_width : q_width + kv_width],
        qkv_total[:, q_width + kv_width :],
        summed[2],
        summed[3],
        gate_up_total[:, :ff_width],
        gate_up_total[:, ff_width:],
        summed[5],
    )


def solution(mesh):
    return jax.shard_map(
        body,
        mesh=mesh,
        in_specs=(
            P("seq", "narrow"),
            P("narrow"),
            P("narrow", "wide"),
            P("narrow", "wide"),
            P("narrow", "wide"),
            P("wide", "narrow"),
            P("narrow"),
            P("narrow", "wide"),
            P("narrow", "wide"),
            P("wide", "narrow"),
            P(),
            P(),
            P("seq", "narrow"),
        ),
        out_specs=(
            P("seq", "narrow"),
            P("seq", "narrow"),
            P("narrow"),
            P("narrow", "wide"),
            P("narrow", "wide"),
            P("narrow", "wide"),
            P("wide", "narrow"),
            P("narrow"),
            P("narrow", "wide"),
            P("narrow", "wide"),
            P("wide", "narrow"),
        ),
        check_vma=False,
    )
```

profile of v0, /device:TPU:0, one launch (start us, length us, event | category | flops | bytes accessed | tf_op | source)
XLA Modules:
  0.0 4983.6 jit_solution(15209267365387991906)
XLA Ops:
  51.3 111.1 %reduce-scatter.5.cloned.1.call-done = f32[1024,768]{1,0:T(8,128)} async-done(((f32[4096,768]{1,0:T(8,128)}), f32[1024,768]{1,0:T(8,128)}) %reduce-scatter.5.cloned.1.call-update) | async-done | bytes 3145744 | tf_op jit(solution)/shard_map/reduce_scatter | solution.py:69
  217.7 410.5 %while.34 = (s32[]{:T(128)}, bf16[8,1024,64]{1,2,0:T(8,128)(2,1)S(1)}, f32[8,1024]{1,0:T(8,128)}, bf16[8,1024,64]{2,1,0:T(8,128)(2,1)}, s32[8]{0:T(128)S(1)}, /*...) while((s32[]{:T(128)}, ...), condition=%wide.region_8.9_spmd.clone.clone, body=%wide.region_5.8_spmd.clone.sunk.clone | while | flops 2239757312 | bytes 111760208 | solution.py:168
  629.6 52.4 %all-gather.8.cloned.1.call-done = bf16[4096,512]{0,1:T(8,128)(2,1)} async-done(((bf16[1024,512]{0,1:T(8,128)(2,1)}), bf16[4096,512]{0,1:T(8,128)(2,1)}) %all-gather.8.cloned.1.call-update) | async-done | bytes 4194320 | tf_op jit(solution)/shard_map/all_gather | solution.py:44
  714.4 266.7 %all-reduce.10.cloned.1.call-done = f32[4096,512]{1,0:T(8,128)} async-done(((f32[4096,512]{1,0:T(8,128)}), f32[4096,512]{1,0:T(8,128)}) %all-reduce.10.cloned.1.call-update) | async-done | bytes 8388624 | tf_op jit(solution)/shard_map/psum | solution.py:40
  1006.9 34.1 fusion.83
  1042.9 229.3 %reduce-scatter.7.cloned.1.call-done = f32[1024,2048]{1,0:T(8,128)} async-done(((f32[4096,2048]{1,0:T(8,128)}), f32[1024,2048]{1,0:T(8,128)}) %reduce-scatter.7.cloned.1.call-update) | async-done | bytes 8388624 | tf_op jit(solution)/shard_map/reduce_scatter | solution.py:69
  1272.2 1120.8 %all-reduce.14.cloned.1.call-done = f32[4096,4096]{1,0:T(8,128)} async-done(((f32[4096,4096]{1,0:T(8,128)}), f32[4096,4096]{1,0:T(8,128)}) %all-reduce.14.cloned.1.call-update) | async-done | bytes 67108880
  2415.0 298.5 %all-gather.12.cloned.1.call-done = bf16[4096,4096]{1,0:T(8,128)(2,1)} async-done(((bf16[1024,4096]{1,0:T(8,128)(2,1)}), bf16[4096,4096]{1,0:T(8,128)(2,1)}) %all-gather.12.cloned.1.call-update) | async-done | bytes 33554448 | tf_op jit(solution)/shard_map/all_gather | solution.py:73
  2738.6 290.9 %all-reduce.12.cloned.1.call-done = f32[4096,512]{1,0:T(8,128)} async-done(((f32[4096,512]{1,0:T(8,128)}), f32[4096,512]{1,0:T(8,128)}) %all-reduce.12.cloned.1.call-update) | async-done | bytes 8388624 | tf_op jit(solution)/shard_map/psum | solution.py:40
  3071.1 83.6 %reduce-scatter.9.cloned.1.call-done = f32[1024,512]{1,0:T(8,128)} async-done(((f32[4096,512]{1,0:T(8,128)}), f32[1024,512]{1,0:T(8,128)}) %reduce-scatter.9.cloned.1.call-update) | async-done | bytes 2097168 | tf_op jit(solution)/shard_map/reduce_scatter | solution.py:69
  3159.0 861.1 %while.35 = (s32[]{:T(128)}, f32[8,1024,64]{1,2,0:T(8,128)}, f32[8,8192,64]{1,2,0:T(8,128)}, f32[8,8192,64]{1,2,0:T(8,128)}, bf16[8,1024,64]{2,1,0:T(8,128)(2,1)...) while((s32[]{:T(128)}, f32[8,1024,64]{1,2,0:T(8,128)}, ...), condition=%wide.region_21.22_spmd.clone.clone, body=%wide.region_19.21_spmd.clone.sunk.clone | while | flops 5478349824 | bytes 344006528 | solution.py:224
  3178.0 28.8 multiply_reduce_fusion.6
  3285.6 28.7 multiply_reduce_fusion.6
  3314.3 27.5 multiply_convert_fusion.9
  3393.1 28.7 multiply_reduce_fusion.6
  3500.6 28.7 multiply_reduce_fusion.6
  3608.2 28.7 multiply_reduce_fusion.6
  3715.8 28.7 multiply_reduce_fusion.6
  3823.3 28.7 multiply_reduce_fusion.6
  3930.9 28.7 multiply_reduce_fusion.6
  4039.5 46.7 reduce-scatter.11.cloned.1.call-done
  4090.9 155.2 %all-gather.10.cloned.1.call-done = bf16[4096,2048]{1,0:T(8,128)(2,1)} async-done(((bf16[1024,2048]{1,0:T(8,128)(2,1)}), bf16[4096,2048]{1,0:T(8,128)(2,1)}) %all-gather.10.cloned.1.call-update) | async-done | bytes 16777232 | tf_op jit(solution)/shard_map/all_gather | solution.py:44
  4289.5 29.1 all-gather.14.cloned.1.call-done
  4375.6 554.8 %all-reduce.16.cloned.1.call-done = (f32[4096,512]{1,0:T(8,128)}, f32[4096,512]{1,0:T(8,128)}) async-done(((f32[4096,512]{1,0:T(8,128)}, f32[4096,512]{1,0:T(8,128)}), (f32[4096,512]{1,0:T(8,128)}, f32[4096,512]{1,0:T(8,128)})) %all-reduce.16.cloned.1.call-update) | async-done | bytes 16777232 | tf_op jit(solution)/shard_map/psum | solution.py:40
  (359 shorter events, 1394.7 us)
Async XLA Ops:
  7.2 683.1 %copy-start = (bf16[2048,512]{1,0:T(8,128)(2,1)S(1)}, bf16[2048,512]{1,0:T(8,128)(2,1)}, u32[]{:S(2)}) copy-start(bf16[2048,512]{1,0:T(8,128)(2,1)} %param.26) | copy-start | bytes 6291460
  7.2 155.2 %reduce-scatter.5.cloned.1.call-start = ((), (), s32[]{:S(2)}) async-start(), calls=%async_computation.4 | async-start | bytes 15728640 | tf_op jit(solution)/shard_map/reduce_scatter | solution.py:69
  42.1 162.9 %all-gather.6.cloned.1.call-start = ((), (), s32[]{:S(2)}) async-start(), calls=%async_computation.5 | async-start | bytes 4718592 | tf_op jit(solution)/shard_map/all_gather | solution.py:142
  43.7 124.9 %copy-start.21 = (s32[8192]{0:T(1024)S(1)}, s32[8192]{0:T(1024)}, u32[]{:S(2)}) copy-start(s32[8192]{0:T(1024)} %param.28) | copy-start | bytes 98308
  47.4 129.0 %copy-start.7 = (f32[1024,64]{0,1:T(8,128)}, f32[1024,64]{0,1:T(8,128)S(1)}, u32[]{:S(2)}) copy-start(f32[1024,64]{0,1:T(8,128)S(1)} %fusion.80) | copy-start | bytes 786436
  168.2 513.9 %all-gather.8.cloned.1.call-start = ((), (), s32[]{:S(2)}) async-start(), calls=%async_computation.6 | async-start | bytes 5242880 | tf_op jit(solution)/shard_map/all_gather | solution.py:44
  629.2 351.9 %all-reduce.10.cloned.1.call-start = ((), (), s32[]{:S(2)}) async-start(), calls=%async_computation.7 | async-start | bytes 16777216 | tf_op jit(solution)/shard_map/psum | solution.py:40
  690.2 582.0 %reduce-scatter.7.cloned.1.call-start = ((), (), s32[]{:S(2)}) async-start(), calls=%async_computation.9 | async-start | bytes 41943040 | tf_op jit(solution)/shard_map/reduce_scatter | solution.py:69
  690.2 2362.8 %copy-start.23 = (pred[4096]{0:T(1024)(128)(4,1)}, pred[4096]{0:T(1024)(128)(4,1)S(1)}, u32[]{:S(2)}) copy-start(pred[4096]{0:T(1024)(128)(4,1)S(1)} %dynamic-slice_compare_fusion) | copy-start | bytes 12292
  708.0 1684.9 %all-reduce.14.cloned.1.call-start = ((), (), s32[]{:S(2)}) async-start(), calls=%async_computation.15 | async-start | bytes 134217728
  714.4 292.4 %copy-start.25 = (f32[512]{0:T(512)S(1)}, f32[512]{0:T(512)}, u32[]{:S(2)}) copy-start(f32[512]{0:T(512)} %param.23) | copy-start | bytes 6148
  1006.9 2046.2 %copy-start.19 = (f32[4096]{0:T(1024)}, f32[4096]{0:T(1024)S(1)}, u32[]{:S(2)}) copy-start(f32[4096]{0:T(1024)S(1)} %add_rsqrt_fusion) | copy-start | bytes 49156
  1041.0 1672.5 %all-gather.12.cloned.1.call-start = ((), (), s32[]{:S(2)}) async-start(), calls=%async_computation.10 | async-start | bytes 41943040 | tf_op jit(solution)/shard_map/all_gather | solution.py:73
  2414.8 614.8 %all-reduce.12.cloned.1.call-start = ((), (), s32[]{:S(2)}) async-start(), calls=%async_computation.11 | async-start | bytes 16777216 | tf_op jit(solution)/shard_map/psum | solution.py:40
  2738.6 416.2 %reduce-scatter.9.cloned.1.call-start = ((), (), s32[]{:S(2)}) async-start(), calls=%async_computation.12 | async-start | bytes 10485760 | tf_op jit(solution)/shard_map/reduce_scatter | solution.py:69
  3071.0 1015.2 %reduce-scatter.11.cloned.1.call-start = ((), (), s32[]{:S(2)}) async-start(), calls=%async_computation.13 | async-start | bytes 4718592 | tf_op jit(solution)/shard_map/reduce_scatter | solution.py:236
  4034.8 211.3 %all-gather.10.cloned.1.call-start = ((), (), s32[]{:S(2)}) async-start(), calls=%async_computation.8 | async-start | bytes 20971520 | tf_op jit(solution)/shard_map/all_gather | solution.py:44
  4035.5 283.1 %all-gather.14.cloned.1.call-start = ((), (), s32[]{:S(2)}) async-start(), calls=%async_computation.14 | async-start | bytes 7864320 | tf_op jit(solution)/shard_map/all_gather | solution.py:73
  4037.3 208.8 %copy-start.24 = (pred[4096]{0:T(1024)(128)(4,1)S(1)}, pred[4096]{0:T(1024)(128)(4,1)}, u32[]{:S(2)}) copy-start(pred[4096]{0:T(1024)(128)(4,1)} %copy-done.23) | copy-start | bytes 12292
  4090.8 170.2 %copy-start.20 = (f32[4096]{0:T(1024)S(1)}, f32[4096]{0:T(1024)}, u32[]{:S(2)}) copy-start(f32[4096]{0:T(1024)} %copy-done.19) | copy-start | bytes 49156
  4090.8 170.2 %copy-start.26 = (f32[512]{0:T(512)S(1)}, f32[512]{0:T(512)}, u32[]{:S(2)}) copy-start(f32[512]{0:T(512)} %param.23) | copy-start | bytes 6148
  4090.8 271.9 %all-reduce.18.cloned.1.call-start = ((), (), s32[]{:S(2)}) async-start(), calls=%async_computation.17 | async-start | bytes 15204352 | tf_op jit(solution)/shard_map/psum | solution.py:253
  4327.7 602.7 %all-reduce.16.cloned.1.call-start = ((), (), s32[]{:S(2)}) async-start(), calls=%async_computation.16 | async-start | bytes 33554432 | tf_op jit(solution)/shard_map/psum | solution.py:40
  4375.6 560.7 %copy-start.30 = (bf16[512]{0:T(512)(128)(2,1)S(1)}, bf16[512]{0:T(512)(128)(2,1)}, u32[]{:S(2)}) copy-start(bf16[512]{0:T(512)(128)(2,1)} %get-tuple-element.396) | copy-start | bytes 3076
  (56 other events, 1228.0 us)
Sparse Core Ops, SparseCore 0:
  42.2 120.1 reduce-scatter.4
  168.3 36.6 all-gather.5
  629.3 52.7 all-gather.7
  690.2 290.8 all-reduce.9
  984.0 288.1 reduce-scatter.6
  1275.9 1116.9 all-reduce.13
  2414.9 298.5 all-gather.11
  2738.7 290.8 all-reduce.11
  3071.1 83.5 reduce-scatter.8
  4034.9 51.2 reduce-scatter.10
  4088.7 157.4 all-gather.9
  4248.4 70.1 all-gather.13
  4327.8 34.8 all-reduce.17
  4366.0 564.4 all-reduce.15
where the time goes:
time: 4990 us; the launch traced here: 4980 us
  waiting for transfers between devices  3270 us (66%)
  matrix products  1040 us (21%)
  other arithmetic  454 us (9%)
  local copies, waits for them, and re-layouts  90.9 us (2%)
  blocking collectives  68.5 us (1%)
    unnamed x15, waiting for transfers between devices  1120 us
    psum x3, waiting for transfers between devices, wide_total(): return lax.psum(values, 'wide')  1110 us
    reduce_scatter x3, waiting for transfers between devices, sum_rows(): lax.psum_scatter(term_rows(), 'narrow', scatter_dimension=0, tiled=True)  424 us
    dot_general x16, matrix products, head_scores(): lax.dot_general(query_one, key_one, (((1,), (1,)), ((), ())), preferred_e...  386 us
    all_gather x2, waiting for transfers between devices, back_rows(): shard_piece = lax.all_gather(grad_rows, 'narrow', axis=0, tiled=True)  328 us
    convert_element_type x8, other arithmetic, head_backward(): score_grad = (attn_prob * (prob_grad - inner_sum)).astype(jnp.bfloat16)  220 us
    all_gather x2, waiting for transfers between devices, gather_rows(): return lax.all_gather(values, 'narrow', axis=0, tiled=True)  208 us
    dot_general x8, matrix products, head_backward(): lax.dot_general(prob_low, grad_one, (((0,), (0,)), ((), ())), preferred_e...  119 us
  transfers between devices with their start and end apart: 14, of which 14 were waited for; matrix products, arithmetic and copies ran while one was open for 4% of the time, Pallas kernels for 0%

commit v1 on v0

--- a/solution.py
+++ b/solution.py
@@ -8,6 +8,19 @@
 EPS = 1e-05
 THETA = 500000.0
 NEG = -1e30
+
+
+def gather_around(x, axis, dim):
+    ways = lax.axis_size(axis)
+    up = [(d, (d + 1) % ways) for d in range(ways)]
+    down = [(d, (d - 1) % ways) for d in range(ways)]
+    earlier, later = ([x], [x])
+    for _ in range(ways // 2):
+        earlier.append(lax.ppermute(earlier[-1], axis, up))
+    for _ in range((ways - 1) // 2):
+        later.append(lax.ppermute(later[-1], axis, down))
+    line = jnp.concatenate([*earlier[::-1], *later[1:]], axis=dim)
+    return jnp.roll(line, (lax.axis_index(axis) - ways // 2) * x.shape[dim], axis=dim)
 
 
 def positions(segment_ids):
@@ -70,7 +83,7 @@
 
 
 def back_rows(grad_rows, weight, inputs):
-    shard_piece = lax.all_gather(grad_rows, "narrow", axis=0, tiled=True)
+    shard_piece = gather_around(grad_rows, "narrow", 0)
     product = lax.dot_general(
         shard_piece, weight, (((1,), (1,)), ((), ())), preferred_element_type=jnp.float32
     )

time: 4990 us -> 5320 us (1.066)
  waiting for transfers between devices: 3270 us -> 3520 us
  local copies, waits for them, and re-layouts: 90.9 us -> 152 us
    ppermute x0 -> x6, waiting for transfers between devices: none -> 552 us  [the longest x4 398 us: gather_around(): earlier.append(lax.ppermute(earlier[-1], axis, up))]
    all_gather x2 -> x0, waiting for transfers between devices: 328 us -> none  [back_rows(): shard_piece = lax.all_gather(grad_rows, 'narrow', axis=0, tiled=True)]
    unnamed x15 -> x13, waiting for transfers between devices: 1120 us -> 1120 us
  transfers between devices with their start and end apart: 14 -> 18, of which waited for: 14 -> 16; matrix products, arithmetic and copies ran while one was open for 4% -> 4% of each run, Pallas kernels for 0% -> 0%
where the time goes in v1:
time: 5320 us; the launch traced here: 5310 us
  waiting for transfers between devices  3520 us (66%)
  matrix products  1040 us (20%)
  other arithmetic  470 us (9%)
  local copies, waits for them, and re-layouts  152 us (3%)
  blocking collectives  68.6 us (1%)
    unnamed x13, waiting for transfers between devices  1120 us
    psum x3, waiting for transfers between devices, wide_total(): return lax.psum(values, 'wide')  1110 us
    reduce_scatter x3, waiting for transfers between devices, sum_rows(): lax.psum_scatter(term_rows(), 'narrow', scatter_dimension=0, tiled=True)  424 us
    ppermute x4, waiting for transfers between devices, gather_around(): earlier.append(lax.ppermute(earlier[-1], axis, up))  398 us
    dot_general x16, matrix products, head_scores(): lax.dot_general(query_one, key_one, (((1,), (1,)), ((), ())), preferred_e...  387 us
    all_gather x2, waiting for transfers between devices, gather_rows(): return lax.all_gather(values, 'narrow', axis=0, tiled=True)  227 us
    convert_element_type x8, other arithmetic, head_backward(): score_grad = (attn_prob * (prob_grad - inner_sum)).astype(jnp.bfloat16)  220 us
    ppermute x2, waiting for transfers between devices, gather_around(): later.append(lax.ppermute(later[-1], axis, down))  155 us
  transfers between devices with their start and end apart: 18, of which 16 were waited for; matrix products, arithmetic and copies ran while one was open for 4% of the time, Pallas kernels for 0%

profile of v1, /device:TPU:0, one launch (start us, length us, event | category | flops | bytes accessed | tf_op | source)
XLA Modules:
  0.0 5312.7 jit_solution(16041763502802789868)
XLA Ops:
  51.3 111.1 %reduce-scatter.5.cloned.1.call-done = f32[1024,768]{1,0:T(8,128)} async-done(((f32[4096,768]{1,0:T(8,128)}), f32[1024,768]{1,0:T(8,128)}) %reduce-scatter.5.cloned.1.call-update) | async-done | bytes 3145744 | tf_op jit(solution)/shard_map/reduce_scatter | solution.py:82
  217.7 410.7 %while.34 = (s32[]{:T(128)}, bf16[8,1024,64]{1,2,0:T(8,128)(2,1)S(1)}, f32[8,1024]{1,0:T(8,128)}, bf16[8,1024,64]{2,1,0:T(8,128)(2,1)}, s32[8]{0:T(128)S(1)}, /*...) while((s32[]{:T(128)}, ...), condition=%wide.region_8.9_spmd.clone.clone, body=%wide.region_5.8_spmd.clone.sunk.clone | while | flops 2239757312 | bytes 111760208 | solution.py:181
  629.6 52.6 all-gather.6.cloned.1.call-done
  715.2 266.2 %all-reduce.10.cloned.1.call-done = f32[4096,512]{1,0:T(8,128)} async-done(((f32[4096,512]{1,0:T(8,128)}), f32[4096,512]{1,0:T(8,128)}) %all-reduce.10.cloned.1.call-update) | async-done | bytes 8388624 | tf_op jit(solution)/shard_map/psum | solution.py:53
  1007.2 34.1 fusion.101
  1043.2 229.2 %reduce-scatter.7.cloned.1.call-done = f32[1024,2048]{1,0:T(8,128)} async-done(((f32[4096,2048]{1,0:T(8,128)}), f32[1024,2048]{1,0:T(8,128)}) %reduce-scatter.7.cloned.1.call-update) | async-done | bytes 8388624 | tf_op jit(solution)/shard_map/reduce_scatter | solution.py:82
  1272.4 1120.8 %all-reduce.14.cloned.1.call-done = f32[4096,4096]{1,0:T(8,128)} async-done(((f32[4096,4096]{1,0:T(8,128)}), f32[4096,4096]{1,0:T(8,128)}) %all-reduce.14.cloned.1.call-update) | async-done | bytes 67108880
  2416.5 182.2 %collective-permute-done = bf16[1024,4096]{1,0:T(8,128)(2,1)} collective-permute-done((bf16[1024,4096]{1,0:T(8,128)(2,1)}, bf16[1024,4096]{1,0:T(8,128)(2,1)}, u32[]{:S(2)}, u32[]{:S(2)}) %collective-permute-start) | collective-permute-done | bytes 8388640 | tf_op jit(solution)/shard_map/ppermute | solution.py:19
  2602.0 181.2 %collective-permute-done.1 = bf16[1024,4096]{1,0:T(8,128)(2,1)} collective-permute-done((bf16[1024,4096]{1,0:T(8,128)(2,1)}, bf16[1024,4096]{1,0:T(8,128)(2,1)}, u32[]{:S(2)}, u32[]{:S(2)}) %collective-permute-start.1) | collective-permute-done | bytes 8388640 | tf_op jit(solution)/shard_map/ppermute | solution.py:19
  2806.6 154.7 %collective-permute-done.2 = bf16[1024,4096]{1,0:T(8,128)(2,1)} collective-permute-done((bf16[1024,4096]{1,0:T(8,128)(2,1)}, bf16[1024,4096]{1,0:T(8,128)(2,1)}, u32[]{:S(2)}, u32[]{:S(2)}) %collective-permute-start.2) | collective-permute-done | bytes 8388640 | tf_op jit(solution)/shard_map/ppermute | solution.py:21
  3025.1 289.9 %all-reduce.12.cloned.1.call-done = f32[4096,512]{1,0:T(8,128)} async-done(((f32[4096,512]{1,0:T(8,128)}), f32[4096,512]{1,0:T(8,128)}) %all-reduce.12.cloned.1.call-update) | async-done | bytes 8388624 | tf_op jit(solution)/shard_map/psum | solution.py:53
  3356.6 83.6 %reduce-scatter.9.cloned.1.call-done = f32[1024,512]{1,0:T(8,128)} async-done(((f32[4096,512]{1,0:T(8,128)}), f32[1024,512]{1,0:T(8,128)}) %reduce-scatter.9.cloned.1.call-update) | async-done | bytes 2097168 | tf_op jit(solution)/shard_map/reduce_scatter | solution.py:82
  3444.5 861.2 %while.35 = (s32[]{:T(128)}, f32[8,1024,64]{1,2,0:T(8,128)}, f32[8,8192,64]{1,2,0:T(8,128)}, f32[8,8192,64]{1,2,0:T(8,128)}, bf16[8,1024,64]{2,1,0:T(8,128)(2,1)...) while((s32[]{:T(128)}, f32[8,1024,64]{1,2,0:T(8,128)}, ...), condition=%wide.region_21.22_spmd.clone.clone, body=%wide.region_19.21_spmd.clone.sunk.clone | while | flops 5478349824 | bytes 344006528 | solution.py:237
  3463.1 28.8 multiply_reduce_fusion.6
  3678.2 28.8 multiply_reduce_fusion.6
  3785.8 28.8 multiply_reduce_fusion.6
  3893.4 28.8 multiply_reduce_fusion.6
  4001.0 28.8 multiply_reduce_fusion.6
  4108.6 28.8 multiply_reduce_fusion.6
  4216.2 28.8 multiply_reduce_fusion.6
  4325.0 46.9 reduce-scatter.11.cloned.1.call-done
  4406.3 34.2 collective-permute-done.3
  4442.1 174.2 %all-gather.8.cloned.1.call-done = bf16[4096,2048]{1,0:T(8,128)(2,1)} async-done(((bf16[1024,2048]{1,0:T(8,128)(2,1)}), bf16[4096,2048]{1,0:T(8,128)(2,1)}) %all-gather.8.cloned.1.call-update) | async-done | bytes 16777232 | tf_op jit(solution)/shard_map/all_gather | solution.py:57
  4704.6 554.8 %all-reduce.16.cloned.1.call-done = (f32[4096,512]{1,0:T(8,128)}, f32[4096,512]{1,0:T(8,128)}) async-done(((f32[4096,512]{1,0:T(8,128)}, f32[4096,512]{1,0:T(8,128)}), (f32[4096,512]{1,0:T(8,128)}, f32[4096,512]{1,0:T(8,128)})) %all-reduce.16.cloned.1.call-update) | async-done | bytes 16777232 | tf_op jit(solution)/shard_map/psum | solution.py:53
  (392 shorter events, 1536.7 us)
Async XLA Ops:
  7.2 683.9 %copy-start = (bf16[2048,512]{1,0:T(8,128)(2,1)S(1)}, bf16[2048,512]{1,0:T(8,128)(2,1)}, u32[]{:S(2)}) copy-start(bf16[2048,512]{1,0:T(8,128)(2,1)} %param.26) | copy-start | bytes 6291460
  7.2 155.2 %reduce-scatter.5.cloned.1.call-start = ((), (), s32[]{:S(2)}) async-start(), calls=%async_computation.4 | async-start | bytes 15728640 | tf_op jit(solution)/shard_map/reduce_scatter | solution.py:82
  42.1 162.9 %all-gather.4.cloned.1.call-start = ((), (), s32[]{:S(2)}) async-start(), calls=%async_computation.5 | async-start | bytes 4718592 | tf_op jit(solution)/shard_map/all_gather | solution.py:155
  168.1 514.1 %all-gather.6.cloned.1.call-start = ((), (), s32[]{:S(2)}) async-start(), calls=%async_computation.6 | async-start | bytes 5242880 | tf_op jit(solution)/shard_map/all_gather | solution.py:57
  629.4 351.9 %all-reduce.10.cloned.1.call-start = ((), (), s32[]{:S(2)}) async-start(), calls=%async_computation.7 | async-start | bytes 16777216 | tf_op jit(solution)/shard_map/psum | solution.py:53
  690.4 582.0 %reduce-scatter.7.cloned.1.call-start = ((), (), s32[]{:S(2)}) async-start(), calls=%async_computation.9 | async-start | bytes 41943040 | tf_op jit(solution)/shard_map/reduce_scatter | solution.py:82
  708.8 1684.4 %all-reduce.14.cloned.1.call-start = ((), (), s32[]{:S(2)}) async-start(), calls=%async_computation.13 | async-start | bytes 134217728
  715.2 292.0 %copy-start.33 = (f32[512]{0:T(512)S(1)}, f32[512]{0:T(512)}, u32[]{:S(2)}) copy-start(f32[512]{0:T(512)} %param.23) | copy-start | bytes 6148
  1007.2 2331.4 %copy-start.26 = (f32[4096]{0:T(1024)}, f32[4096]{0:T(1024)S(1)}, u32[]{:S(2)}) copy-start(f32[4096]{0:T(1024)S(1)} %add_rsqrt_fusion) | copy-start | bytes 49156
  1041.4 2273.7 %all-reduce.12.cloned.1.call-start = ((), (), s32[]{:S(2)}) async-start(), calls=%async_computation.10 | async-start | bytes 16777216 | tf_op jit(solution)/shard_map/psum | solution.py:53
  2415.0 183.6 %collective-permute-start = (bf16[1024,4096]{1,0:T(8,128)(2,1)}, bf16[1024,4096]{1,0:T(8,128)(2,1)}, u32[]{:S(2)}, u32[]{:S(2)}) collective-permute-start(bf16[1024,4096]{1,0:T(8,128)(2,1)} %pad_maximum_fusion), channel_id=1, source_target_pairs={{0,4},{4,8},{8,12},{12,0},{1,5},{5,9},{9,13},{13,1},{2,6},{6,10},{... | collective-permute-start | bytes 25165832 | tf_op jit(solution)/shard_map/ppermute | solution.py:19
  2598.6 184.6 %collective-permute-start.1 = (bf16[1024,4096]{1,0:T(8,128)(2,1)}, bf16[1024,4096]{1,0:T(8,128)(2,1)}, u32[]{:S(2)}, u32[]{:S(2)}) collective-permute-start(bf16[1024,4096]{1,0:T(8,128)(2,1)} %collective-permute-done), channel_id=1, source_target_pairs={{0,4},{4,8},{8,12},{12,0},{1,5},{5,9},{9,13},{13,1},{2,6},{6,10},{... | collective-permute-start | bytes 25165832 | tf_op jit(solution)/shard_map/ppermute | solution.py:19
  2599.1 362.2 %collective-permute-start.2 = (bf16[1024,4096]{1,0:T(8,128)(2,1)}, bf16[1024,4096]{1,0:T(8,128)(2,1)}, u32[]{:S(2)}, u32[]{:S(2)}) collective-permute-start(bf16[1024,4096]{1,0:T(8,128)(2,1)} %pad_maximum_fusion), channel_id=1, source_target_pairs={{0,12},{4,0},{8,4},{12,8},{1,13},{5,1},{9,5},{13,9},{2,14},{6,2},{... | collective-permute-start | bytes 25165832 | tf_op jit(solution)/shard_map/ppermute | solution.py:21
  3025.1 313.5 %copy-start.31 = (pred[4096]{0:T(1024)(128)(4,1)S(1)}, pred[4096]{0:T(1024)(128)(4,1)}, u32[]{:S(2)}) copy-start(pred[4096]{0:T(1024)(128)(4,1)} %copy-done.30) | copy-start | bytes 12292
  3025.1 415.2 %reduce-scatter.9.cloned.1.call-start = ((), (), s32[]{:S(2)}) async-start(), calls=%async_computation.11 | async-start | bytes 10485760 | tf_op jit(solution)/shard_map/reduce_scatter | solution.py:82
  3356.5 1015.3 %reduce-scatter.11.cloned.1.call-start = ((), (), s32[]{:S(2)}) async-start(), calls=%async_computation.12 | async-start | bytes 4718592 | tf_op jit(solution)/shard_map/reduce_scatter | solution.py:249
  4320.4 295.9 %all-gather.8.cloned.1.call-start = ((), (), s32[]{:S(2)}) async-start(), calls=%async_computation.8 | async-start | bytes 20971520 | tf_op jit(solution)/shard_map/all_gather | solution.py:57
  4320.9 370.7 %all-reduce.18.cloned.1.call-start = ((), (), s32[]{:S(2)}) async-start(), calls=%async_computation.15 | async-start | bytes 15204352 | tf_op jit(solution)/shard_map/psum | solution.py:266
  4376.5 239.8 %copy-start.32 = (pred[4096]{0:T(1024)(128)(4,1)S(1)}, pred[4096]{0:T(1024)(128)(4,1)}, u32[]{:S(2)}) copy-start(pred[4096]{0:T(1024)(128)(4,1)} %copy-done.30) | copy-start | bytes 12292
  4376.5 64.0 %collective-permute-start.3 = (bf16[1024,768]{0,1:T(8,128)(2,1)}, bf16[1024,768]{0,1:T(8,128)(2,1)}, u32[]{:S(2)}, u32[]{:S(2)}) collective-permute-start(bf16[1024,768]{0,1:T(8,128)(2,1)} %pad_maximum_fusion.2), channel_id=1, source_target_pairs={{0,4},{4,8},{8,12},{12,0},{1,5},{5,9},{9,13},{13,1},{2,6},{6,10},{... | collective-permute-start | bytes 4718600 | tf_op jit(solution)/shard_map/ppermute | solution.py:19
  4405.5 235.6 %collective-permute-start.5 = (bf16[1024,768]{0,1:T(8,128)(2,1)}, bf16[1024,768]{0,1:T(8,128)(2,1)}, u32[]{:S(2)}, u32[]{:S(2)}) collective-permute-start(bf16[1024,768]{0,1:T(8,128)(2,1)} %pad_maximum_fusion.2), channel_id=1, source_target_pairs={{0,12},{4,0},{8,4},{12,8},{1,13},{5,1},{9,5},{13,9},{2,14},{6,2},{... | collective-permute-start | bytes 4718600 | tf_op jit(solution)/shard_map/ppermute | solution.py:21
  4440.4 197.3 %collective-permute-start.4 = (bf16[1024,768]{0,1:T(8,128)(2,1)}, bf16[1024,768]{0,1:T(8,128)(2,1)}, u32[]{:S(2)}, u32[]{:S(2)}) collective-permute-start(bf16[1024,768]{0,1:T(8,128)(2,1)} %collective-permute-done.3), channel_id=1, source_target_pairs={{0,4},{4,8},{8,12},{12,0},{1,5},{5,9},{9,13},{13,1},{2,6},{6,10},{... | collective-permute-start | bytes 4718600 | tf_op jit(solution)/shard_map/ppermute | solution.py:19
  4657.5 601.9 %all-reduce.16.cloned.1.call-start = ((), (), s32[]{:S(2)}) async-start(), calls=%async_computation.14 | async-start | bytes 33554432 | tf_op jit(solution)/shard_map/psum | solution.py:53
  4704.6 560.7 %copy-start.38 = (bf16[512]{0:T(512)(128)(2,1)S(1)}, bf16[512]{0:T(512)(128)(2,1)}, u32[]{:S(2)}) copy-start(bf16[512]{0:T(512)(128)(2,1)} %get-tuple-element.396) | copy-start | bytes 3076
  (66 other events, 1531.1 us)
Sparse Core Ops, SparseCore 0:
  42.2 120.1 reduce-scatter.4
  168.3 36.6 all-gather.3
  629.5 52.6 all-gather.5
  690.5 290.8 all-reduce.9
  984.3 288.1 reduce-scatter.6
  1276.2 1116.9 all-reduce.13
  3025.2 289.8 all-reduce.11
  3356.6 83.5 reduce-scatter.8
  4320.5 51.3 reduce-scatter.10
  4374.1 242.0 all-gather.7
  4657.6 34.0 all-reduce.17
  4694.9 564.4 all-reduce.15
